TPU v7x, 32 devices: a whole 2x2x4 slice. The times are simulated.
32 devices in a mesh: dp: 4 (over z), mp: 8 (over y, x, core).
Axes of the slice: x: 2, y: 2, z: 4, core: 2. Of those that a mesh axis runs over, the one named last changes fastest.
Arguments:
- block_input: bfloat16 [8192, 2048], P(('dp', 'mp')), may hold values from -6 to 6
- out_cotangent: bfloat16 [8192, 2048], P(('dp', 'mp')), may hold values from -6 to 6
- objective: int32 [16], P('dp'), may hold values from 0 to 1, as said below
- prefix_len: int32 [16], P('dp'), may hold values from 64 to 511
- target_mask: int32 [8192], P(('dp', 'mp')), may hold values from 0 to 1, as said below
- qkv_weight: float32 [2048, 3, 2048], P('dp', None, 'mp'), may hold values from -0.125 to 0.125
- out_weight: float32 [2048, 2048], P('mp', 'dp'), may hold values from -3 to 3
- gateup_weight: float32 [2048, 2, 5472], P('dp', None, 'mp'), may hold values from -0.125 to 0.125
- down_weight: float32 [5472, 2048], P('mp', 'dp'), may hold values from -0.625 to 0.625
- norm_params: float32 [4, 2048], replicated, as said below
- qkv_first: float32 [2048, 3, 2048], P('dp', None, 'mp'), may hold values from -0.125 to 0.125
- out_first: float32 [2048, 2048], P('mp', 'dp'), may hold values from -0.005859375 to 0.005859375
- gateup_first: float32 [2048, 2, 5472], P('dp', None, 'mp'), may hold values from -0.09375 to 0.09375
- down_first: float32 [5472, 2048], P('mp', 'dp'), may hold values from -0.013671875 to 0.013671875
- norm_first: float32 [4, 2048], replicated, may hold values from -0.21875 to 0.21875
- qkv_second: float32 [2048, 3, 2048], P('dp', None, 'mp'), may hold values from 3.0517578e-05 to 0.00048828125
- out_second: float32 [2048, 2048], P('mp', 'dp'), may hold values from 7.080078e-08 to 1.1230469e-06
- gateup_second: float32 [2048, 2, 5472], P('dp', None, 'mp'), may hold values from 1.953125e-05 to 0.0003125
- down_second: float32 [5472, 2048], P('mp', 'dp'), may hold values from 4.3945312e-07 to 7.080078e-06
- norm_second: float32 [4, 2048], replicated, may hold values from 0.00012207031 to 0.001953125
Outputs:
- block_output: bfloat16 [8192, 2048], P(('dp', 'mp'))
- input_grad: float32 [8192, 2048], P(('dp', 'mp'))
- qkv_new: float32 [2048, 3, 2048], P('dp', None, 'mp')
- qkv_first_new: float32 [2048, 3, 2048], P('dp', None, 'mp')
- qkv_second_new: float32 [2048, 3, 2048], P('dp', None, 'mp')
- out_new: float32 [2048, 2048], P('mp', 'dp')
- out_first_new: float32 [2048, 2048], P('mp', 'dp')
- out_second_new: float32 [2048, 2048], P('mp', 'dp')
- gateup_new: float32 [2048, 2, 5472], P('dp', None, 'mp')
- gateup_first_new: float32 [2048, 2, 5472], P('dp', None, 'mp')
- gateup_second_new: float32 [2048, 2, 5472], P('dp', None, 'mp')
- down_new: float32 [5472, 2048], P('mp', 'dp')
- down_first_new: float32 [5472, 2048], P('mp', 'dp')
- down_second_new: float32 [5472, 2048], P('mp', 'dp')
- norm_new: float32 [4, 2048], replicated
- norm_first_new: float32 [4, 2048], replicated
- norm_second_new: float32 [4, 2048], replicated
Inputs may be any that keep to these rules, and one draw needn't show every extreme that they name: `objective`: at least one sequence of each kind. `target_mask`: the last residue of every sequence is a target. `norm_params`: rows 0 and 2 are the gains of the first and second norm, rows 1 and 3 their biases.
All inputs are finite; a program needn't handle non-finite values.
Results may differ from a plain program's by a relative error of at most 0.024.
Values may be sent and summed in bfloat16 or wider, within the bound.
No kernel may reach another device: no remote copies, remote signals or barrier semaphores. Data moves between devices by JAX's collectives and lax.ppermute only.
A program may use at most 256 MiB of HBM per device.

v0:
```python
import jax
import jax.numpy as jnp
from jax import lax
from jax.sharding import PartitionSpec as P

D = 2048
HD = 128
FF = 5461
FF_PAD = 5472
STEP = 5
deep_alpha = 48.0**0.5
norm_eps = 1e-05
masked_score = -1e30
rope_base = 10000.0
beta_one = 0.5
beta_two = 0.5
adam_eps = 1e-08
decay_rate = 0.1


def rope_tables(seq_len, head_dim):
    position = jnp.arange(seq_len, dtype=jnp.float32)
    freqs = rope_base ** (-jnp.arange(0, head_dim, 2, dtype=jnp.float32) / head_dim)
    angles = position[:, None] * freqs[None, :]
    return (jnp.cos(angles), jnp.sin(angles))


def rotate(values, cosine, sine_table):
    half_dim = values.shape[-1] // 2
    first_half = values[..., :half_dim]
    second_half = values[..., half_dim:]
    cos_b = cosine[:, None, :]
    sin_b = sine_table[:, None, :]
    return jnp.concatenate(
        [first_half * cos_b - second_half * sin_b, second_half * cos_b + first_half * sin_b], -1
    )


def norm_forward(hidden, norm_gain, norm_bias):
    row_mean = jnp.mean(hidden, -1, keepdims=True)
    centred = hidden - row_mean
    variance = jnp.mean(centred * centred, -1, keepdims=True)
    inv_std = lax.rsqrt(variance + norm_eps)
    normed = centred * inv_std
    return (normed * norm_gain + norm_bias, normed, inv_std)


def norm_backward(grad_rows, normed, inv_std, norm_gain):
    grad_normed = grad_rows * norm_gain
    mean_grad = jnp.mean(grad_normed, -1, keepdims=True)
    mean_proj = jnp.mean(grad_normed * normed, -1, keepdims=True)
    grad_in = inv_std * (grad_normed - mean_grad - normed * mean_proj)
    return (grad_in, jnp.sum(grad_rows * normed, 0), jnp.sum(grad_rows, 0))


def adamw(weight, gradient, first_moment, second, step_rate):
    first_new = beta_one * first_moment + (1.0 - beta_one) * gradient
    second_new = beta_two * second + (1.0 - beta_two) * gradient * gradient
    first_hat = first_new / (1.0 - beta_one**STEP)
    second_hat = second_new / (1.0 - beta_two**STEP)
    weight_new = weight - step_rate * (
        first_hat / (jnp.sqrt(second_hat) + adam_eps) + decay_rate * weight
    )
    return (weight_new, first_new, second_new)


def local(
    block_input,
    out_cotangent,
    objective,
    prefix_len,
    target_mask,
    qkv_weight,
    out_weight,
    gateup_weight,
    down_weight,
    norm_params,
    qkv_first,
    out_first,
    gateup_first,
    down_first,
    norm_first,
    qkv_second,
    out_second,
    gateup_second,
    down_second,
    norm_second,
):
    mp_count = lax.axis_size("mp")
    mp_index = lax.axis_index("mp")
    own_rows = block_input.shape[0]
    seq_count = objective.shape[0]
    group_rows = own_rows * mp_count
    seq_len = group_rows // seq_count
    local_dim = qkv_weight.shape[2]
    local_heads = local_dim // HD
    local_units = gateup_weight.shape[2]
    score_scale = HD ** (-0.5)
    row_start = mp_index * own_rows
    qkv_full, out_full, gateup_full, down_full = (
        lax.all_gather(qkv_weight.astype(jnp.bfloat16), "dp", axis=0, tiled=True),
        lax.all_gather(out_weight.astype(jnp.bfloat16), "dp", axis=1, tiled=True),
        lax.all_gather(gateup_weight.astype(jnp.bfloat16), "dp", axis=0, tiled=True),
        lax.all_gather(down_weight.astype(jnp.bfloat16), "dp", axis=1, tiled=True),
    )
    input_all = lax.all_gather(block_input, "mp", axis=0, tiled=True)
    projected = jnp.einsum("td,dce->tce", input_all, qkv_full, preferred_element_type=jnp.float32)
    shaped = projected.reshape(seq_count, seq_len, 3, local_heads, HD)
    cosine, sine_table = rope_tables(seq_len, HD)
    query_rows = rotate(shaped[:, :, 0], cosine, sine_table).astype(jnp.bfloat16)
    key_rows = rotate(shaped[:, :, 1], cosine, sine_table).astype(jnp.bfloat16)
    value_rows = shaped[:, :, 2].astype(jnp.bfloat16)
    row_index = jnp.arange(seq_len)[:, None]
    col_index = jnp.arange(seq_len)[None, :]
    visible = (
        (objective[:, None, None] > 0)
        | (col_index[None] < prefix_len[:, None, None])
        | (col_index <= row_index)[None]
    )
    scores = (
        jnp.einsum("sihe,sjhe->shij", query_rows, key_rows, preferred_element_type=jnp.float32)
        * score_scale
    )
    scores = jnp.where(visible[:, None], scores, masked_score)
    row_max = jnp.max(scores, -1, keepdims=True)
    exp_scores = jnp.exp(scores - row_max)
    row_total = jnp.sum(exp_scores, -1, keepdims=True)
    soft_weights = exp_scores / row_total
    log_total = row_max + jnp.log(row_total)
    attended = jnp.einsum(
        "shij,sjhe->sihe",
        soft_weights.astype(jnp.bfloat16),
        value_rows,
        preferred_element_type=jnp.float32,
    )
    attended_low = attended.reshape(group_rows, local_dim).astype(jnp.bfloat16)
    attn_part = jnp.dot(attended_low, out_full, preferred_element_type=jnp.float32)
    attn_total = lax.psum(attn_part, "mp")
    hidden_all = deep_alpha * input_all.astype(jnp.float32) + attn_total
    middle_all, _, _ = norm_forward(hidden_all, norm_params[0], norm_params[1])
    middle_low = middle_all.astype(jnp.bfloat16)
    hidden_one = lax.dynamic_slice_in_dim(hidden_all, row_start, own_rows, 0)
    middle = lax.dynamic_slice_in_dim(middle_all, row_start, own_rows, 0)
    live_units = (mp_index * local_units + jnp.arange(local_units) < FF).astype(jnp.float32)
    gate_up = jnp.einsum("td,dcf->tcf", middle_low, gateup_full, preferred_element_type=jnp.float32)
    hidden_low = (jax.nn.gelu(gate_up[:, 0]) * gate_up[:, 1] * live_units).astype(jnp.bfloat16)
    ffn_part = jnp.dot(hidden_low, down_full, preferred_element_type=jnp.float32)
    ffn_total = lax.psum(ffn_part.astype(jnp.bfloat16), "mp").astype(jnp.float32)
    ffn_own = lax.dynamic_slice_in_dim(ffn_total, row_start, own_rows, 0)
    hidden_two = deep_alpha * middle + ffn_own
    output_rows, normed_two, inv_two = norm_forward(hidden_two, norm_params[2], norm_params[3])
    mask_f32 = target_mask.astype(jnp.float32)
    grad_rows = out_cotangent.astype(jnp.float32) * mask_f32[:, None]
    grad_two, gain_two, bias_two = norm_backward(grad_rows, normed_two, inv_two, norm_params[2])
    ffn_back = lax.all_gather(grad_two.astype(jnp.bfloat16), "mp", axis=0, tiled=True)
    gate_again = jnp.einsum(
        "td,dcf->tcf", middle_low, gateup_full, preferred_element_type=jnp.float32
    )
    gate_act, gelu_pull = jax.vjp(jax.nn.gelu, gate_again[:, 0])
    up_part = gate_again[:, 1]
    hidden_again = (gate_act * up_part * live_units).astype(jnp.bfloat16)
    grad_hidden = (
        jnp.einsum("td,fd->tf", ffn_back, down_full, preferred_element_type=jnp.float32)
        * live_units
    )
    down_grad = jnp.einsum("tf,td->fd", hidden_again, ffn_back, preferred_element_type=jnp.float32)
    grad_gate = gelu_pull(grad_hidden * up_part)[0]
    grad_up = grad_hidden * gate_act
    grad_gateup = jnp.stack([grad_gate, grad_up], 1).astype(jnp.bfloat16)
    middle_part = jnp.einsum(
        "tcf,dcf->td", grad_gateup, gateup_full, preferred_element_type=jnp.float32
    )
    gateup_grad = jnp.einsum(
        "td,tcf->dcf", middle_low, grad_gateup, preferred_element_type=jnp.float32
    )
    grad_middle = (
        lax.psum_scatter(
            middle_part.astype(jnp.bfloat16), "mp", scatter_dimension=0, tiled=True
        ).astype(jnp.float32)
        + deep_alpha * grad_two
    )
    _, normed_one, inv_one = norm_forward(hidden_one, norm_params[0], norm_params[1])
    grad_one, gain_one, bias_one = norm_backward(grad_middle, normed_one, inv_one, norm_params[0])
    attn_back = lax.all_gather(grad_one.astype(jnp.bfloat16), "mp", axis=0, tiled=True)
    grad_attended = jnp.einsum(
        "td,ed->te", attn_back, out_full, preferred_element_type=jnp.float32
    ).astype(jnp.bfloat16)
    grad_attended = grad_attended.reshape(seq_count, seq_len, local_heads, HD)
    out_grad = jnp.einsum("te,td->ed", attended_low, attn_back, preferred_element_type=jnp.float32)
    scores_again = (
        jnp.einsum("sihe,sjhe->shij", query_rows, key_rows, preferred_element_type=jnp.float32)
        * score_scale
    )
    scores_again = jnp.where(visible[:, None], scores_again, masked_score)
    soft_again = jnp.exp(scores_again - log_total)
    grad_soft = jnp.einsum(
        "sihe,sjhe->shij", grad_attended, value_rows, preferred_element_type=jnp.float32
    )
    value_grad = jnp.einsum(
        "shij,sihe->sjhe",
        soft_again.astype(jnp.bfloat16),
        grad_attended,
        preferred_element_type=jnp.float32,
    )
    row_dot = jnp.sum(soft_again * grad_soft, -1, keepdims=True)
    grad_scores = (soft_again * (grad_soft - row_dot)).astype(jnp.bfloat16)
    query_grad = (
        jnp.einsum("shij,sjhe->sihe", grad_scores, key_rows, preferred_element_type=jnp.float32)
        * score_scale
    )
    key_grad = (
        jnp.einsum("shij,sihe->sjhe", grad_scores, query_rows, preferred_element_type=jnp.float32)
        * score_scale
    )
    query_lin = rotate(query_grad, cosine, -sine_table)
    key_lin = rotate(key_grad, cosine, -sine_table)
    grad_proj = (
        jnp.stack([query_lin, key_lin, value_grad], 2)
        .astype(jnp.bfloat16)
        .reshape(group_rows, 3, local_dim)
    )
    input_part = jnp.einsum("tce,dce->td", grad_proj, qkv_full, preferred_element_type=jnp.float32)
    qkv_grad = jnp.einsum("td,tce->dce", input_all, grad_proj, preferred_element_type=jnp.float32)
    input_raw = (
        lax.psum_scatter(
            input_part.astype(jnp.bfloat16), "mp", scatter_dimension=0, tiled=True
        ).astype(jnp.float32)
        + deep_alpha * grad_one
    )
    qkv_grad, out_grad, gateup_grad, down_grad = (
        lax.psum_scatter(
            qkv_grad.astype(jnp.bfloat16), "dp", scatter_dimension=0, tiled=True
        ).astype(jnp.float32),
        lax.psum_scatter(
            out_grad.astype(jnp.bfloat16), "dp", scatter_dimension=1, tiled=True
        ).astype(jnp.float32),
        lax.psum_scatter(
            gateup_grad.astype(jnp.bfloat16), "dp", scatter_dimension=0, tiled=True
        ).astype(jnp.float32),
        lax.psum_scatter(
            down_grad.astype(jnp.bfloat16), "dp", scatter_dimension=1, tiled=True
        ).astype(jnp.float32),
    )
    norm_grad = jnp.stack([gain_one, bias_one, gain_two, bias_two], 0)
    norm_grad, target_count = lax.psum((norm_grad, jnp.sum(mask_f32)), ("dp", "mp"))
    rate_list = (D ** (-0.5), 0.5, D ** (-0.5), (FF_PAD // 64) ** (-0.5), 0.4)
    qkv_res = adamw(qkv_weight, qkv_grad / target_count, qkv_first, qkv_second, rate_list[0])
    out_res = adamw(out_weight, out_grad / target_count, out_first, out_second, rate_list[1])
    gateup_res = adamw(
        gateup_weight, gateup_grad / target_count, gateup_first, gateup_second, rate_list[2]
    )
    down_res = adamw(down_weight, down_grad / target_count, down_first, down_second, rate_list[3])
    norm_res = adamw(norm_params, norm_grad / target_count, norm_first, norm_second, rate_list[4])
    return (
        output_rows.astype(jnp.bfloat16),
        input_raw / target_count,
        qkv_res[0],
        qkv_res[1],
        qkv_res[2],
        out_res[0],
        out_res[1],
        out_res[2],
        gateup_res[0],
        gateup_res[1],
        gateup_res[2],
        down_res[0],
        down_res[1],
        down_res[2],
        norm_res[0],
        norm_res[1],
        norm_res[2],
    )


def solution(mesh):
    return jax.shard_map(
        local,
        mesh=mesh,
        in_specs=(
            P(("dp", "mp"), None),
            P(("dp", "mp"), None),
            P("dp"),
            P("dp"),
            P(("dp", "mp")),
            P("dp", None, "mp"),
            P("mp", "dp"),
            P("dp", None, "mp"),
            P("mp", "dp"),
            P(),
            P("dp", None, "mp"),
            P("mp", "dp"),
            P("dp", None, "mp"),
            P("mp", "dp"),
            P(),
            P("dp", None, "mp"),
            P("mp", "dp"),
            P("dp", None, "mp"),
            P("mp", "dp"),
            P(),
        ),
        out_specs=(
            P(("dp", "mp"), None),
            P(("dp", "mp"), None),
            P("dp", None, "mp"),
            P("dp", None, "mp"),
            P("dp", None, "mp"),
            P("mp", "dp"),
            P("mp", "dp"),
            P("mp", "dp"),
            P("dp", None, "mp"),
            P("dp", None, "mp"),
            P("dp", None, "mp"),
            P("mp", "dp"),
            P("mp", "dp"),
            P("mp", "dp"),
            P(),
            P(),
            P(),
        ),
        check_vma=False,
    )
```

profile of v0, /device:TPU:0, one launch (start us, length us, event | category | flops | bytes accessed | tf_op | source)
XLA Modules:
  0.0 1279.1 jit_solution(2433256142239264889)
XLA Ops:
  14.7 61.7 %all-gather.10.cloned.1.call-done = bf16[2048,3,256]{2,0,1:T(8,128)(2,1)} async-done(((bf16[512,3,256]{2,0,1:T(8,128)(2,1)}), bf16[2048,3,256]{2,0,1:T(8,128)(2,1)}) %all-gather.10.cloned.1.call-update) | async-done | bytes 3145744 | tf_op jit(solution)/shard_map/all_gather | solution.py:101
  76.4 54.8 %all-gather.8.cloned.1.call-done = bf16[2048,2048]{1,0:T(8,128)(2,1)} async-done(((bf16[256,2048]{1,0:T(8,128)(2,1)}), bf16[2048,2048]{1,0:T(8,128)(2,1)}) %all-gather.8.cloned.1.call-update) | async-done | bytes 8388624 | tf_op jit(solution)/shard_map/all_gather | solution.py:106
  131.2 11.6 fusion.6
  142.8 8.3 reshape.239
  151.1 3.9 fusion.82
  155.0 3.3 slice.73
  173.4 11.4 copy.105
  184.8 9.7 fusion.51
  200.8 211.6 %all-reduce.4.cloned.1.call-done = f32[2048,2048]{1,0:T(8,128)} async-done(((f32[2048,2048]{1,0:T(8,128)}), f32[2048,2048]{1,0:T(8,128)}) %all-reduce.4.cloned.1.call-update) | async-done | bytes 16777232 | tf_op jit(solution)/shard_map/psum | solution.py:138
  412.5 16.0 %fusion.81 = (f32[2048]{0:T(1024)S(1)}, f32[2048,2048]{1,0:T(8,128)}) fusion(f32[2048,2048]{1,0:T(8,128)} %all-reduce.4.cloned.1.call-done, bf16[2048,2048]{1,0:T(8,128)(2,1)} %all-gather.8.cloned.1.call-done), kind=kLoop, calls=%fused_computation.166 | loop fusion | flops 16775168 | bytes 41951232 | tf_op jit(solution)/shard_map/reduce_sum | solution.py:40
  428.5 7.7 multiply_reduce_fusion
  436.2 12.2 multiply_add_fusion
  448.5 69.6 %all-gather.14.cloned.1.call-done = bf16[2048,2,684]{0,1,2:T(2,128)(2,1)} async-done(((bf16[512,2,684]{0,1,2:T(2,128)(2,1)}), bf16[2048,2,684]{0,1,2:T(2,128)(2,1)}) %all-gather.14.cloned.1.call-update) | async-done | bytes 5603344 | tf_op jit(solution)/shard_map/all_gather | solution.py:103
  518.1 22.3 %fusion.2 = f32[2048,2,684]{0,2,1:T(8,128)} fusion(bf16[2048,2,684]{0,1,2:T(2,128)(2,1)} %all-gather.14.cloned.1.call-done, f32[2048,2048]{1,0:T(8,128)} %multiply_add_fusion), kind=kOutput, calls=%fused_computation.7 | convolution fusion | flops 11479810048 | bytes 33587200 | tf_op jit(solution)/shard_map/td,dcf->tcf/dot_general | solution.py:145
  540.3 5.5 multiply_convert_fusion.2
  545.8 30.5 %all-gather.16.cloned.1.call-done = bf16[684,2048]{1,0:T(8,128)(2,1)} async-done(((bf16[684,512]{1,0:T(8,128)(2,1)}), bf16[684,2048]{1,0:T(8,128)(2,1)}) %all-gather.16.cloned.1.call-update) | async-done | bytes 2801680 | tf_op jit(solution)/shard_map/all_gather | solution.py:104
  576.3 11.2 convolution_convert_fusion
  588.2 124.4 %all-reduce.6.cloned.1.call-done = bf16[2048,2048]{1,0:T(8,128)(2,1)} async-done(((bf16[2048,2048]{1,0:T(8,128)(2,1)}), bf16[2048,2048]{1,0:T(8,128)(2,1)}) %all-reduce.6.cloned.1.call-update) | async-done | bytes 8388624 | tf_op jit(solution)/shard_map/psum | solution.py:148
  719.2 54.5 %all-gather.18.cloned.1.call-done = bf16[2048,2048]{1,0:T(8,128)(2,1)} async-done(((bf16[256,2048]{1,0:T(8,128)(2,1)}), bf16[2048,2048]{1,0:T(8,128)(2,1)}) %all-gather.18.cloned.1.call-update) | async-done | bytes 8388624 | tf_op jit(solution)/shard_map/all_gather | solution.py:155
  773.7 15.4 %fusion.36 = (bf16[2048,1,684]{0,2,1:T(8,128)(2,1)S(1)}, bf16[2048,1,684]{0,2,1:T(8,128)(2,1)S(1)}) fusion(f32[2048,2,684]{0,2,1:T(8,128)} %fusion.2, f32[684]{0:T(1024)S(1)} %fusion.66, bf16[2048,2048]{1,0:T(8,128)(2,1)} %all-gather.18.cloned.1.call-done, bf16[684,2048]{1,0:T(8,128)(2,1)} %all-gather.16.cloned.1.call-done), kind=kOutput, calls=%fused_computation.56 | convolution fusion | flops 5772828672 | bytes 28002992 | tf_op jit(solution)/shard_map/td,fd->tf/dot_general | solution.py:163
  791.6 17.9 %bitcast_convert_fusion.1 = bf16[2048,2048]{1,0:T(8,128)(2,1)} fusion(bf16[2048,2,684]{0,1,2:T(2,128)(2,1)} %all-gather.14.cloned.1.call-done, bf16[2048,1,684]{0,2,1:T(8,128)(2,1)S(1)} %get-tuple-element.102, bf16[2048,1,684]{0,2,1:T(8,128)(2,1)S(1)} %get-tuple-element.101), kind=kOutput, calls=%fused_computation.1 | convolution fusion | flops 11482611712 | bytes 19595264 | tf_op jit(solution)/shard_map/tcf,dcf->td/dot_general | solution.py:170
  813.5 67.7 %reduce-scatter.7.cloned.1.call-done = bf16[256,2048]{1,0:T(8,128)(2,1)} async-done(((bf16[2048,2048]{1,0:T(8,128)(2,1)}), bf16[256,2048]{1,0:T(8,128)(2,1)}) %reduce-scatter.7.cloned.1.call-update) | async-done | bytes 1048592 | tf_op jit(solution)/shard_map/reduce_scatter | solution.py:177
  884.2 4.1 fusion.78
  888.4 18.6 %fusion.19 = bf16[2048,2,684]{0,2,1:T(8,128)(2,1)} fusion(f32[2048,2048]{1,0:T(8,128)} %multiply_add_fusion, bf16[2048,1,684]{0,2,1:T(8,128)(2,1)} %copy-done.49, bf16[2048,1,684]{0,2,1:T(8,128)(2,1)} %copy-done.48), kind=kOutput, calls=%fused_computation.39 | convolution fusion | flops 11493818368 | bytes 27983872 | tf_op jit(solution)/shard_map/td,tcf->dcf/dot_general | solution.py:173
  908.8 10.6 convolution_convert_fusion.1
  920.2 22.6 %all-gather.20.cloned.1.call-done = bf16[2048,2048]{1,0:T(8,128)(2,1)} async-done(((bf16[256,2048]{1,0:T(8,128)(2,1)}), bf16[2048,2048]{1,0:T(8,128)(2,1)}) %all-gather.20.cloned.1.call-update) | async-done | bytes 8388624 | tf_op jit(solution)/shard_map/all_gather | solution.py:184
  942.7 5.8 convolution_convert_fusion.3
  949.6 6.0 fusion.46
  959.4 4.5 multiply_reduce_fusion.1
  964.0 4.8 multiply_convert_fusion
  984.3 6.8 convolution_convert_fusion.2
  993.3 12.0 fusion.31
  1007.1 10.8 bitcast_convert_fusion
  1027.8 41.6 %all-reduce = (f32[]{:T(128)}, f32[4,2048]{1,0:T(4,128)S(1)}) all-reduce(f32[]{:T(128)} %convert_reduce_fusion, f32[4,2048]{1,0:T(4,128)S(1)} %pad_maximum_fusion.11), channel_id=1, replica_groups=mesh['dp'=4,'mp'=8] {'dp','mp'}, use_global_device_ids=true, to_apply=%region_18.19 | all-reduce | flops 8193 | bytes 65544 | tf_op jit(solution)/shard_map/psum | solution.py:245
  1069.5 5.2 multiply_subtract_fusion
  1074.7 3.7 copy.133
  1078.4 3.7 copy.134
  1082.2 3.7 copy.135
  1087.2 16.2 %reduce-scatter.17.cloned.1.call-done = bf16[684,512]{1,0:T(8,128)(2,1)} async-done(((bf16[684,2048]{1,0:T(8,128)(2,1)}), bf16[684,512]{1,0:T(8,128)(2,1)}) %reduce-scatter.17.cloned.1.call-update) | async-done | bytes 700432 | tf_op jit(solution)/shard_map/reduce_scatter | solution.py:240
  1103.5 5.1 multiply_subtract_fusion.2
  1108.6 24.2 %reduce-scatter.13.cloned.1.call-done = bf16[256,512]{1,0:T(8,128)(2,1)} async-done(((bf16[256,2048]{1,0:T(8,128)(2,1)}), bf16[256,512]{1,0:T(8,128)(2,1)}) %reduce-scatter.13.cloned.1.call-update) | async-done | bytes 262160 | tf_op jit(solution)/shard_map/reduce_scatter | solution.py:234
  1132.8 3.6 multiply_subtract_fusion.3
  1136.4 57.5 %reduce-scatter.11.cloned.1.call-done = bf16[512,3,256]{0,2,1:T(8,128)(2,1)} async-done(((bf16[2048,3,256]{0,2,1:T(8,128)(2,1)}), bf16[512,3,256]{0,2,1:T(8,128)(2,1)}) %reduce-scatter.11.cloned.1.call-update) | async-done | bytes 786448 | tf_op jit(solution)/shard_map/reduce_scatter | solution.py:231
  1193.9 5.5 multiply_subtract_fusion.1
  1202.4 3.2 copy.131
  1205.6 3.3 copy.132
  1208.9 59.7 %reduce-scatter.9.cloned.1.call-done = bf16[256,2048]{1,0:T(8,128)(2,1)} async-done(((bf16[2048,2048]{1,0:T(8,128)(2,1)}), bf16[256,2048]{1,0:T(8,128)(2,1)}) %reduce-scatter.9.cloned.1.call-update) | async-done | bytes 1048592 | tf_op jit(solution)/shard_map/reduce_scatter | solution.py:225
  1268.6 3.5 add_divide_fusion
  (192 shorter events, 86.6 us)
Async XLA Ops:
  7.2 3.3 copy-start.28
  7.2 6.0 copy-start.47
  7.2 6.0 copy-start.46
  7.2 69.1 %all-gather.10.cloned.1.call-start = ((), (), s32[]{:S(2)}) async-start(), calls=%async_computation.7 | async-start | bytes 3932160 | tf_op jit(solution)/shard_map/all_gather | solution.py:101
  9.7 121.5 %all-gather.8.cloned.1.call-start = ((), (), s32[]{:S(2)}) async-start(), calls=%async_computation.6 | async-start | bytes 9437184 | tf_op jit(solution)/shard_map/all_gather | solution.py:106
  10.5 174.4 %all-gather.12.cloned.1.call-start = ((), (), s32[]{:S(2)}) async-start(), calls=%async_computation.8 | async-start | bytes 1310720 | tf_op jit(solution)/shard_map/all_gather | solution.py:102
  11.3 401.2 %all-reduce.4.cloned.1.call-start = ((), (), s32[]{:S(2)}) async-start(), calls=%async_computation.9 | async-start | bytes 33554432 | tf_op jit(solution)/shard_map/psum | solution.py:138
  13.2 150.0 %copy-start.26 = (f32[512,64]{1,0:T(8,128)}, f32[512,64]{1,0:T(8,128)S(1)}, u32[]{:S(2)}) copy-start(f32[512,64]{1,0:T(8,128)S(1)} %get-tuple-element.124) | copy-start | bytes 393220
  160.7 8.2 copy-start.14
  164.7 3.0 copy-start.5
  164.7 3.0 copy-start.7
  164.7 3.0 copy-start.9
  164.7 3.0 copy-start.11
  167.7 3.3 copy-start
  167.7 3.4 copy-start.34
  184.8 9.7 copy-start.1
  194.5 323.5 %all-gather.14.cloned.1.call-start = ((), (), s32[]{:S(2)}) async-start(), calls=%async_computation.10 | async-start | bytes 7004160 | tf_op jit(solution)/shard_map/all_gather | solution.py:103
  198.4 377.9 %all-gather.16.cloned.1.call-start = ((), (), s32[]{:S(2)}) async-start(), calls=%async_computation.11 | async-start | bytes 3522560 | tf_op jit(solution)/shard_map/all_gather | solution.py:104
  200.7 511.8 %all-reduce.6.cloned.1.call-start = ((), (), s32[]{:S(2)}) async-start(), calls=%async_computation.12 | async-start | bytes 16777216 | tf_op jit(solution)/shard_map/psum | solution.py:148
  545.8 41.6 %copy-start.24 = (bf16[2048,684]{0,1:T(8,128)(2,1)}, bf16[2048,684]{0,1:T(8,128)(2,1)S(1)}, u32[]{:S(2)}) copy-start(bf16[2048,684]{0,1:T(8,128)(2,1)S(1)} %multiply_convert_fusion.2) | copy-start | bytes 8404996
  587.5 186.2 %all-gather.18.cloned.1.call-start = ((), (), s32[]{:S(2)}) async-start(), calls=%async_computation.13 | async-start | bytes 9437184 | tf_op jit(solution)/shard_map/all_gather | solution.py:155
  588.2 127.0 %copy-start.20 = (bf16[256,2048]{1,0:T(8,128)(2,1)S(1)}, bf16[256,2048]{1,0:T(8,128)(2,1)}, u32[]{:S(2)}) copy-start(bf16[256,2048]{1,0:T(8,128)(2,1)} %param.21) | copy-start | bytes 3145732
  719.1 162.0 %reduce-scatter.7.cloned.1.call-start = ((), (), s32[]{:S(2)}) async-start(), calls=%async_computation.14 | async-start | bytes 9437184 | tf_op jit(solution)/shard_map/reduce_scatter | solution.py:177
  809.5 133.2 %all-gather.20.cloned.1.call-start = ((), (), s32[]{:S(2)}) async-start(), calls=%async_computation.15 | async-start | bytes 9437184 | tf_op jit(solution)/shard_map/all_gather | solution.py:184
  881.2 3.0 copy-start.21
  888.3 181.1 %reduce-scatter.15.cloned.1.call-start = ((), (), s32[]{:S(2)}) async-start(), calls=%async_computation.19 | async-start | bytes 7045120 | tf_op jit(solution)/shard_map/reduce_scatter | solution.py:237
  907.0 196.4 %reduce-scatter.17.cloned.1.call-start = ((), (), s32[]{:S(2)}) async-start(), calls=%async_computation.20 | async-start | bytes 3522560 | tf_op jit(solution)/shard_map/reduce_scatter | solution.py:240
  919.4 23.3 %copy-start.30 = (bf16[256,2048]{1,0:T(8,128)(2,1)S(1)}, bf16[256,2048]{1,0:T(8,128)(2,1)}, u32[]{:S(2)}) copy-start(bf16[256,2048]{1,0:T(8,128)(2,1)} %all-gather.12.cloned.1.call-done) | copy-start | bytes 3145732
  919.5 213.3 %reduce-scatter.13.cloned.1.call-start = ((), (), s32[]{:S(2)}) async-start(), calls=%async_computation.18 | async-start | bytes 1310720 | tf_op jit(solution)/shard_map/reduce_scatter | solution.py:234
  955.6 3.8 copy-start.15
  963.9 4.8 copy-start.10
  963.9 4.8 copy-start.12
  979.4 4.9 copy-start.2
  984.3 6.9 copy-start.22
  991.1 202.7 %reduce-scatter.11.cloned.1.call-start = ((), (), s32[]{:S(2)}) async-start(), calls=%async_computation.17 | async-start | bytes 3932160 | tf_op jit(solution)/shard_map/reduce_scatter | solution.py:231
  1005.3 263.3 %reduce-scatter.9.cloned.1.call-start = ((), (), s32[]{:S(2)}) async-start(), calls=%async_computation.16 | async-start | bytes 9437184 | tf_op jit(solution)/shard_map/reduce_scatter | solution.py:225
  1019.4 4.8 copy-start.45
  1019.4 5.4 copy-start.40
  1019.4 5.4 copy-start.41
  1021.0 48.5 %copy-start.4 = (f32[512,2,684]{0,1,2:T(2,128)S(1)}, f32[512,2,684]{0,1,2:T(2,128)}, u32[]{:S(2)}) copy-start(f32[512,2,684]{0,1,2:T(2,128)} %param.27) | copy-start | bytes 8404996
  1082.1 3.7 copy-start.37
  1082.1 3.7 copy-start.42
  1082.1 3.7 copy-start.43
  1082.1 21.3 %copy-start.19 = (f32[684,512]{1,0:T(8,128)S(1)}, f32[684,512]{1,0:T(8,128)}, u32[]{:S(2)}) copy-start(f32[684,512]{1,0:T(8,128)} %param.28) | copy-start | bytes 4202500
  1082.1 21.3 %copy-start.29 = (f32[684,512]{1,0:T(8,128)S(1)}, f32[684,512]{1,0:T(8,128)}, u32[]{:S(2)}) copy-start(f32[684,512]{1,0:T(8,128)} %param.33) | copy-start | bytes 4202500
  1108.6 85.3 %copy-start.17 = (f32[512,3,256]{0,2,1:T(8,128)S(1)}, f32[512,3,256]{0,2,1:T(8,128)}, u32[]{:S(2)}) copy-start(f32[512,3,256]{0,2,1:T(8,128)} %copy.125) | copy-start | bytes 4718596
  1108.6 85.3 %copy-start.18 = (f32[512,3,256]{0,2,1:T(8,128)S(1)}, f32[512,3,256]{0,2,1:T(8,128)}, u32[]{:S(2)}) copy-start(f32[512,3,256]{0,2,1:T(8,128)} %copy.121) | copy-start | bytes 4718596
  1202.4 66.2 %copy-start.13 = (f32[256,2048]{1,0:T(8,128)S(1)}, f32[256,2048]{1,0:T(8,128)}, u32[]{:S(2)}) copy-start(f32[256,2048]{1,0:T(8,128)} %get-tuple-element.94) | copy-start | bytes 6291460
  (17 other events, 26.7 us)
Sparse Core Ops, SparseCore 0:
  10.2 66.1 all-gather.9
  78.3 52.8 all-gather.7
  133.3 27.9 all-gather.11
  194.6 217.7 all-reduce.3
  414.4 103.5 all-gather.13
  520.0 56.2 all-gather.15
  587.6 124.8 all-reduce.5
  719.3 54.3 all-gather.17
  809.6 71.4 reduce-scatter.6
  888.5 54.2 all-gather.19
  945.1 100.1 reduce-scatter.14
  1047.4 55.9 reduce-scatter.16
  1105.7 26.9 reduce-scatter.12
  1134.9 58.8 reduce-scatter.10
  1197.2 71.3 reduce-scatter.8
where the time goes:
time: 1290 us; the launch traced here: 1280 us
  waiting for transfers between devices  856 us (66%)
  matrix products  171 us (13%)
  other arithmetic  105 us (8%)
  local copies, waits for them, and re-layouts  89.7 us (7%)
  blocking collectives  41.6 us (3%)
  between operations  15 us (1%)
    psum x1, waiting for transfers between devices, local(): attn_total = lax.psum(attn_part, 'mp')  212 us
    psum x1, waiting for transfers between devices, local(): lax.psum(ffn_part.astype(jnp.bfloat16), 'mp').astype(jnp.float32)  124 us
    all_gather x1, waiting for transfers between devices, local(): lax.all_gather(gateup_weight.astype(jnp.bfloat16), 'dp', axis=0, tiled=True)  69.6 us
    reduce_scatter x1, waiting for transfers between devices, local(): lax.psum_scatter(middle_part.astype(jnp.bfloat16), 'mp', scatter_dimensio...  67.7 us
    all_gather x1, waiting for transfers between devices, local(): lax.all_gather(qkv_weight.astype(jnp.bfloat16), 'dp', axis=0, tiled=True)  61.7 us
    reduce_scatter x1, waiting for transfers between devices, local(): lax.psum_scatter(input_part.astype(jnp.bfloat16), 'mp', scatter_dimension...  59.7 us
    reduce_scatter x1, waiting for transfers between devices, local(): lax.psum_scatter(qkv_grad.astype(jnp.bfloat16), 'dp', scatter_dimension=0...  57.5 us
    all_gather x1, waiting for transfers between devices, local(): input_all = lax.all_gather(block_input, 'mp', axis=0, tiled=True)  54.8 us
  transfers between devices with their start and end apart: 15, of which 13 were waited for; matrix products, arithmetic and copies ran while one was open for 22% of the time, Pallas kernels for 0%

commit v1 on v0

--- a/solution.py
+++ b/solution.py
@@ -145,7 +145,12 @@
     gate_up = jnp.einsum("td,dcf->tcf", middle_low, gateup_full, preferred_element_type=jnp.float32)
     hidden_low = (jax.nn.gelu(gate_up[:, 0]) * gate_up[:, 1] * live_units).astype(jnp.bfloat16)
     ffn_part = jnp.dot(hidden_low, down_full, preferred_element_type=jnp.float32)
-    ffn_total = lax.psum(ffn_part.astype(jnp.bfloat16), "mp").astype(jnp.float32)
+
+    def resolve_series(inp, dev_axis="mp"):
+        long_array = jnp.sum(lax.all_gather(inp, axis_name=dev_axis), 0)
+        return long_array
+
+    ffn_total = resolve_series(ffn_part.astype(jnp.bfloat16)).astype(jnp.float32)
     ffn_own = lax.dynamic_slice_in_dim(ffn_total, row_start, own_rows, 0)
     hidden_two = deep_alpha * middle + ffn_own
     output_rows, normed_two, inv_two = norm_forward(hidden_two, norm_params[2], norm_params[3])

time: 1290 us -> 1480 us (1.15)
  waiting for transfers between devices: 856 us -> 1030 us
  other arithmetic: 105 us -> 130 us
    all_gather x0 -> x1, waiting for transfers between devices: none -> 301 us  [resolve_series(): long_array = jnp.sum(lax.all_gather(inp, axis_name=dev_axis), 0)]
    psum x1 -> x0, waiting for transfers between devices: 124 us -> none  [local(): lax.psum(ffn_part.astype(jnp.bfloat16), 'mp').astype(jnp.float32)]
    reduce_sum x0 -> x1, other arithmetic: none -> 25.9 us  [resolve_series(): long_array = jnp.sum(lax.all_gather(inp, axis_name=dev_axis), 0)]
  transfers between devices with their start and end apart: 15 -> 15, of which waited for: 13 -> 13; matrix products, arithmetic and copies ran while one was open for 22% -> 18% of each run, Pallas kernels for 0% -> 0%
where the time goes in v1:
time: 1480 us; the launch traced here: 1470 us
  waiting for transfers between devices  1030 us (70%)
  matrix products  171 us (12%)
  other arithmetic  130 us (9%)
  local copies, waits for them, and re-layouts  79.1 us (5%)
  blocking collectives  41.5 us (3%)
  between operations  15 us (1%)
    all_gather x1, waiting for transfers between devices, resolve_series(): long_array = jnp.sum(lax.all_gather(inp, axis_name=dev_axis), 0)  301 us
    psum x1, waiting for transfers between devices, local(): attn_total = lax.psum(attn_part, 'mp')  212 us
    all_gather x1, waiting for transfers between devices, local(): lax.all_gather(gateup_weight.astype(jnp.bfloat16), 'dp', axis=0, tiled=True)  69.5 us
    reduce_scatter x1, waiting for transfers between devices, local(): lax.psum_scatter(middle_part.astype(jnp.bfloat16), 'mp', scatter_dimensio...  67.7 us
    all_gather x1, waiting for transfers between devices, local(): lax.all_gather(qkv_weight.astype(jnp.bfloat16), 'dp', axis=0, tiled=True)  61.7 us
    reduce_scatter x1, waiting for transfers between devices, local(): lax.psum_scatter(input_part.astype(jnp.bfloat16), 'mp', scatter_dimension...  59.7 us
    reduce_scatter x1, waiting for transfers between devices, local(): lax.psum_scatter(qkv_grad.astype(jnp.bfloat16), 'dp', scatter_dimension=0...  57.6 us
    all_gather x1, waiting for transfers between devices, local(): input_all = lax.all_gather(block_input, 'mp', axis=0, tiled=True)  54.8 us
  transfers between devices with their start and end apart: 15, of which 13 were waited for; matrix products, arithmetic and copies ran while one was open for 18% of the time, Pallas kernels for 0%

profile of v1, /device:TPU:0, one launch (start us, length us, event | category | flops | bytes accessed | tf_op | source)
XLA Modules:
  0.0 1471.0 jit_solution(1026437086258964539)
XLA Ops:
  14.7 61.7 %all-gather.12.cloned.1.call-done = bf16[2048,3,256]{2,0,1:T(8,128)(2,1)} async-done(((bf16[512,3,256]{2,0,1:T(8,128)(2,1)}), bf16[2048,3,256]{2,0,1:T(8,128)(2,1)}) %all-gather.12.cloned.1.call-update) | async-done | bytes 3145744 | tf_op jit(solution)/shard_map/all_gather | solution.py:101
  76.4 54.8 %all-gather.10.cloned.1.call-done = bf16[2048,2048]{1,0:T(8,128)(2,1)} async-done(((bf16[256,2048]{1,0:T(8,128)(2,1)}), bf16[2048,2048]{1,0:T(8,128)(2,1)}) %all-gather.10.cloned.1.call-update) | async-done | bytes 8388624 | tf_op jit(solution)/shard_map/all_gather | solution.py:106
  131.2 11.6 fusion.6
  142.8 8.3 reshape.239
  151.1 3.9 fusion.82
  155.0 3.3 slice.73
  174.5 9.7 fusion.51
  190.5 211.6 %all-reduce.3.cloned.1.call-done = f32[2048,2048]{1,0:T(8,128)} async-done(((f32[2048,2048]{1,0:T(8,128)}), f32[2048,2048]{1,0:T(8,128)}) %all-reduce.3.cloned.1.call-update) | async-done | bytes 16777232 | tf_op jit(solution)/shard_map/psum | solution.py:138
  402.1 16.0 %fusion.81 = (f32[2048]{0:T(1024)S(1)}, f32[2048,2048]{1,0:T(8,128)}) fusion(f32[2048,2048]{1,0:T(8,128)} %all-reduce.3.cloned.1.call-done, bf16[2048,2048]{1,0:T(8,128)(2,1)} %all-gather.10.cloned.1.call-done), kind=kLoop, calls=%fused_computation.166 | loop fusion | flops 16775168 | bytes 41951232 | tf_op jit(solution)/shard_map/reduce_sum | solution.py:40
  418.1 7.7 multiply_reduce_fusion
  425.8 12.3 multiply_add_fusion
  438.1 69.5 %all-gather.16.cloned.1.call-done = bf16[2048,2,684]{0,1,2:T(2,128)(2,1)} async-done(((bf16[512,2,684]{0,1,2:T(2,128)(2,1)}), bf16[2048,2,684]{0,1,2:T(2,128)(2,1)}) %all-gather.16.cloned.1.call-update) | async-done | bytes 5603344 | tf_op jit(solution)/shard_map/all_gather | solution.py:103
  507.7 22.2 %fusion.2 = f32[2048,2,684]{0,2,1:T(8,128)} fusion(bf16[2048,2,684]{0,1,2:T(2,128)(2,1)} %all-gather.16.cloned.1.call-done, f32[2048,2048]{1,0:T(8,128)} %multiply_add_fusion), kind=kOutput, calls=%fused_computation.7 | convolution fusion | flops 11479810048 | bytes 33587200 | tf_op jit(solution)/shard_map/td,dcf->tcf/dot_general | solution.py:145
  529.9 5.5 multiply_convert_fusion.2
  535.4 30.5 %all-gather.18.cloned.1.call-done = bf16[684,2048]{1,0:T(8,128)(2,1)} async-done(((bf16[684,512]{1,0:T(8,128)(2,1)}), bf16[684,2048]{1,0:T(8,128)(2,1)}) %all-gather.18.cloned.1.call-update) | async-done | bytes 2801680 | tf_op jit(solution)/shard_map/all_gather | solution.py:104
  565.9 11.1 convolution_convert_fusion
  577.7 300.9 %all-gather.24.cloned.1.call-done = bf16[16384,2048]{1,0:T(8,128)(2,1)} async-done(((bf16[2048,2048]{1,0:T(8,128)(2,1)}), bf16[16384,2048]{1,0:T(8,128)(2,1)}) %all-gather.24.cloned.1.call-update) | async-done | bytes 67108880 | tf_op jit(solution)/shard_map/all_gather | solution.py:150
  878.6 25.9 %reduce_sum.168 = bf16[2048,2048]{1,0:T(8,128)(2,1)} reduce(bf16[8,2048,2048]{2,1,0:T(8,128)(2,1)} %bitcast.10, bf16[]{:T(256)} %constant.49.clone.1), dimensions={0}, to_apply=%region_5.6 | reduce | flops 29360128 | bytes 75497472 | tf_op jit(solution)/shard_map/reduce_sum | solution.py:150
  911.3 54.4 %all-gather.20.cloned.1.call-done = bf16[2048,2048]{1,0:T(8,128)(2,1)} async-done(((bf16[256,2048]{1,0:T(8,128)(2,1)}), bf16[2048,2048]{1,0:T(8,128)(2,1)}) %all-gather.20.cloned.1.call-update) | async-done | bytes 8388624 | tf_op jit(solution)/shard_map/all_gather | solution.py:160
  965.6 15.5 %fusion.36 = (bf16[2048,1,684]{0,2,1:T(8,128)(2,1)S(1)}, bf16[2048,1,684]{0,2,1:T(8,128)(2,1)S(1)}) fusion(f32[2048,2,684]{0,2,1:T(8,128)} %fusion.2, f32[684]{0:T(1024)S(1)} %fusion.66, bf16[2048,2048]{1,0:T(8,128)(2,1)} %all-gather.20.cloned.1.call-done, bf16[684,2048]{1,0:T(8,128)(2,1)} %all-gather.18.cloned.1.call-done), kind=kOutput, calls=%fused_computation.56 | convolution fusion | flops 5772828672 | bytes 28002992 | tf_op jit(solution)/shard_map/td,fd->tf/dot_general | solution.py:168
  983.6 17.9 %bitcast_convert_fusion.1 = bf16[2048,2048]{1,0:T(8,128)(2,1)} fusion(bf16[2048,2,684]{0,1,2:T(2,128)(2,1)} %all-gather.16.cloned.1.call-done, bf16[2048,1,684]{0,2,1:T(8,128)(2,1)S(1)} %get-tuple-element.102, bf16[2048,1,684]{0,2,1:T(8,128)(2,1)S(1)} %get-tuple-element.101), kind=kOutput, calls=%fused_computation.1 | convolution fusion | flops 11482611712 | bytes 19595264 | tf_op jit(solution)/shard_map/tcf,dcf->td/dot_general | solution.py:175
  1005.5 67.7 %reduce-scatter.7.cloned.1.call-done = bf16[256,2048]{1,0:T(8,128)(2,1)} async-done(((bf16[2048,2048]{1,0:T(8,128)(2,1)}), bf16[256,2048]{1,0:T(8,128)(2,1)}) %reduce-scatter.7.cloned.1.call-update) | async-done | bytes 1048592 | tf_op jit(solution)/shard_map/reduce_scatter | solution.py:182
  1076.2 4.1 fusion.78
  1080.4 18.7 %fusion.19 = bf16[2048,2,684]{0,2,1:T(8,128)(2,1)} fusion(f32[2048,2048]{1,0:T(8,128)} %multiply_add_fusion, bf16[2048,1,684]{0,2,1:T(8,128)(2,1)} %copy-done.49, bf16[2048,1,684]{0,2,1:T(8,128)(2,1)} %copy-done.48), kind=kOutput, calls=%fused_computation.39 | convolution fusion | flops 11493818368 | bytes 27983872 | tf_op jit(solution)/shard_map/td,tcf->dcf/dot_general | solution.py:178
  1100.9 10.7 convolution_convert_fusion.1
  1112.3 22.5 %all-gather.22.cloned.1.call-done = bf16[2048,2048]{1,0:T(8,128)(2,1)} async-done(((bf16[256,2048]{1,0:T(8,128)(2,1)}), bf16[2048,2048]{1,0:T(8,128)(2,1)}) %all-gather.22.cloned.1.call-update) | async-done | bytes 8388624 | tf_op jit(solution)/shard_map/all_gather | solution.py:189
  1134.8 5.8 convolution_convert_fusion.3
  1141.6 6.0 fusion.46
  1151.4 4.5 multiply_reduce_fusion.1
  1156.0 4.8 multiply_convert_fusion
  1176.3 6.8 convolution_convert_fusion.2
  1185.3 12.0 fusion.31
  1199.2 10.8 bitcast_convert_fusion
  1219.8 41.5 %all-reduce = (f32[]{:T(128)}, f32[4,2048]{1,0:T(4,128)S(1)}) all-reduce(f32[]{:T(128)} %convert_reduce_fusion, f32[4,2048]{1,0:T(4,128)S(1)} %pad_maximum_fusion.11), channel_id=1, replica_groups=mesh['dp'=4,'mp'=8] {'dp','mp'}, use_global_device_ids=true, to_apply=%region_18.19 | all-reduce | flops 8193 | bytes 65544 | tf_op jit(solution)/shard_map/psum | solution.py:250
  1261.4 5.2 multiply_subtract_fusion
  1266.6 3.7 copy.133
  1270.3 3.7 copy.134
  1274.0 3.7 copy.135
  1279.1 16.4 %reduce-scatter.17.cloned.1.call-done = bf16[684,512]{1,0:T(8,128)(2,1)} async-done(((bf16[684,2048]{1,0:T(8,128)(2,1)}), bf16[684,512]{1,0:T(8,128)(2,1)}) %reduce-scatter.17.cloned.1.call-update) | async-done | bytes 700432 | tf_op jit(solution)/shard_map/reduce_scatter | solution.py:245
  1295.4 5.1 multiply_subtract_fusion.2
  1300.5 24.2 %reduce-scatter.13.cloned.1.call-done = bf16[256,512]{1,0:T(8,128)(2,1)} async-done(((bf16[256,2048]{1,0:T(8,128)(2,1)}), bf16[256,512]{1,0:T(8,128)(2,1)}) %reduce-scatter.13.cloned.1.call-update) | async-done | bytes 262160 | tf_op jit(solution)/shard_map/reduce_scatter | solution.py:239
  1324.7 3.5 multiply_subtract_fusion.3
  1328.2 57.6 %reduce-scatter.11.cloned.1.call-done = bf16[512,3,256]{0,2,1:T(8,128)(2,1)} async-done(((bf16[2048,3,256]{0,2,1:T(8,128)(2,1)}), bf16[512,3,256]{0,2,1:T(8,128)(2,1)}) %reduce-scatter.11.cloned.1.call-update) | async-done | bytes 786448 | tf_op jit(solution)/shard_map/reduce_scatter | solution.py:236
  1385.8 5.4 multiply_subtract_fusion.1
  1394.3 3.2 copy.131
  1397.5 3.3 copy.132
  1400.9 59.7 %reduce-scatter.9.cloned.1.call-done = bf16[256,2048]{1,0:T(8,128)(2,1)} async-done(((bf16[2048,2048]{1,0:T(8,128)(2,1)}), bf16[256,2048]{1,0:T(8,128)(2,1)}) %reduce-scatter.9.cloned.1.call-update) | async-done | bytes 1048592 | tf_op jit(solution)/shard_map/reduce_scatter | solution.py:230
  1460.6 3.5 add_divide_fusion
  (193 shorter events, 87.5 us)
Async XLA Ops:
  7.2 3.3 copy-start.28
  7.2 6.0 copy-start.47
  7.2 6.0 copy-start.46
  7.2 69.1 %all-gather.12.cloned.1.call-start = ((), (), s32[]{:S(2)}) async-start(), calls=%async_computation.7 | async-start | bytes 3932160 | tf_op jit(solution)/shard_map/all_gather | solution.py:101
  9.7 121.5 %all-gather.10.cloned.1.call-start = ((), (), s32[]{:S(2)}) async-start(), calls=%async_computation.6 | async-start | bytes 9437184 | tf_op jit(solution)/shard_map/all_gather | solution.py:106
  10.5 164.0 %all-gather.14.cloned.1.call-start = ((), (), s32[]{:S(2)}) async-start(), calls=%async_computation.8 | async-start | bytes 1310720 | tf_op jit(solution)/shard_map/all_gather | solution.py:102
  11.3 390.8 %all-reduce.3.cloned.1.call-start = ((), (), s32[]{:S(2)}) async-start(), calls=%async_computation.9 | async-start | bytes 33554432 | tf_op jit(solution)/shard_map/psum | solution.py:138
  13.2 150.0 %copy-start.26 = (f32[512,64]{1,0:T(8,128)}, f32[512,64]{1,0:T(8,128)S(1)}, u32[]{:S(2)}) copy-start(f32[512,64]{1,0:T(8,128)S(1)} %get-tuple-element.124) | copy-start | bytes 393220
  160.7 8.2 copy-start.14
  164.7 3.0 copy-start.5
  164.7 3.0 copy-start.7
  164.7 3.0 copy-start.9
  164.7 3.0 copy-start.11
  167.7 3.3 copy-start
  167.7 3.4 copy-start.34
  174.4 9.7 copy-start.1
  184.2 323.5 %all-gather.16.cloned.1.call-start = ((), (), s32[]{:S(2)}) async-start(), calls=%async_computation.10 | async-start | bytes 7004160 | tf_op jit(solution)/shard_map/all_gather | solution.py:103
  188.0 377.9 %all-gather.18.cloned.1.call-start = ((), (), s32[]{:S(2)}) async-start(), calls=%async_computation.11 | async-start | bytes 3522560 | tf_op jit(solution)/shard_map/all_gather | solution.py:104
  190.4 688.3 %all-gather.24.cloned.1.call-start = ((), (), s32[]{:S(2)}) async-start(), calls=%async_computation.20 | async-start | bytes 75497472 | tf_op jit(solution)/shard_map/all_gather | solution.py:150
  535.4 41.6 %copy-start.24 = (bf16[2048,684]{0,1:T(8,128)(2,1)}, bf16[2048,684]{0,1:T(8,128)(2,1)S(1)}, u32[]{:S(2)}) copy-start(bf16[2048,684]{0,1:T(8,128)(2,1)S(1)} %multiply_convert_fusion.2) | copy-start | bytes 8404996
  577.1 388.6 %all-gather.20.cloned.1.call-start = ((), (), s32[]{:S(2)}) async-start(), calls=%async_computation.12 | async-start | bytes 9437184 | tf_op jit(solution)/shard_map/all_gather | solution.py:160
  904.6 2.7 copy-start.20
  911.2 161.9 %reduce-scatter.7.cloned.1.call-start = ((), (), s32[]{:S(2)}) async-start(), calls=%async_computation.13 | async-start | bytes 9437184 | tf_op jit(solution)/shard_map/reduce_scatter | solution.py:182
  1001.5 133.3 %all-gather.22.cloned.1.call-start = ((), (), s32[]{:S(2)}) async-start(), calls=%async_computation.14 | async-start | bytes 9437184 | tf_op jit(solution)/shard_map/all_gather | solution.py:189
  1073.2 3.0 copy-start.21
  1080.4 181.0 %reduce-scatter.15.cloned.1.call-start = ((), (), s32[]{:S(2)}) async-start(), calls=%async_computation.18 | async-start | bytes 7045120 | tf_op jit(solution)/shard_map/reduce_scatter | solution.py:242
  1099.1 196.3 %reduce-scatter.17.cloned.1.call-start = ((), (), s32[]{:S(2)}) async-start(), calls=%async_computation.19 | async-start | bytes 3522560 | tf_op jit(solution)/shard_map/reduce_scatter | solution.py:245
  1111.5 23.2 %copy-start.30 = (bf16[256,2048]{1,0:T(8,128)(2,1)S(1)}, bf16[256,2048]{1,0:T(8,128)(2,1)}, u32[]{:S(2)}) copy-start(bf16[256,2048]{1,0:T(8,128)(2,1)} %all-gather.14.cloned.1.call-done) | copy-start | bytes 3145732
  1111.5 213.2 %reduce-scatter.13.cloned.1.call-start = ((), (), s32[]{:S(2)}) async-start(), calls=%async_computation.17 | async-start | bytes 1310720 | tf_op jit(solution)/shard_map/reduce_scatter | solution.py:239
  1147.6 3.8 copy-start.15
  1155.9 4.8 copy-start.10
  1156.0 4.8 copy-start.12
  1171.4 4.9 copy-start.2
  1176.3 6.9 copy-start.22
  1183.1 202.7 %reduce-scatter.11.cloned.1.call-start = ((), (), s32[]{:S(2)}) async-start(), calls=%async_computation.16 | async-start | bytes 3932160 | tf_op jit(solution)/shard_map/reduce_scatter | solution.py:236
  1197.3 263.3 %reduce-scatter.9.cloned.1.call-start = ((), (), s32[]{:S(2)}) async-start(), calls=%async_computation.15 | async-start | bytes 9437184 | tf_op jit(solution)/shard_map/reduce_scatter | solution.py:230
  1211.4 4.8 copy-start.45
  1211.4 5.4 copy-start.40
  1211.4 5.4 copy-start.41
  1213.0 48.4 %copy-start.4 = (f32[512,2,684]{0,1,2:T(2,128)S(1)}, f32[512,2,684]{0,1,2:T(2,128)}, u32[]{:S(2)}) copy-start(f32[512,2,684]{0,1,2:T(2,128)} %param.27) | copy-start | bytes 8404996
  1274.0 3.7 copy-start.37
  1274.0 3.7 copy-start.42
  1274.0 3.7 copy-start.43
  1274.0 21.4 %copy-start.19 = (f32[684,512]{1,0:T(8,128)S(1)}, f32[684,512]{1,0:T(8,128)}, u32[]{:S(2)}) copy-start(f32[684,512]{1,0:T(8,128)} %param.28) | copy-start | bytes 4202500
  1274.0 21.4 %copy-start.29 = (f32[684,512]{1,0:T(8,128)S(1)}, f32[684,512]{1,0:T(8,128)}, u32[]{:S(2)}) copy-start(f32[684,512]{1,0:T(8,128)} %param.33) | copy-start | bytes 4202500
  1300.5 85.3 %copy-start.17 = (f32[512,3,256]{0,2,1:T(8,128)S(1)}, f32[512,3,256]{0,2,1:T(8,128)}, u32[]{:S(2)}) copy-start(f32[512,3,256]{0,2,1:T(8,128)} %copy.125) | copy-start | bytes 4718596
  1300.5 85.3 %copy-start.18 = (f32[512,3,256]{0,2,1:T(8,128)S(1)}, f32[512,3,256]{0,2,1:T(8,128)}, u32[]{:S(2)}) copy-start(f32[512,3,256]{0,2,1:T(8,128)} %copy.121) | copy-start | bytes 4718596
  1394.3 66.3 %copy-start.13 = (f32[256,2048]{1,0:T(8,128)S(1)}, f32[256,2048]{1,0:T(8,128)}, u32[]{:S(2)}) copy-start(f32[256,2048]{1,0:T(8,128)} %get-tuple-element.94) | copy-start | bytes 6291460
  (17 other events, 26.5 us)
Sparse Core Ops, SparseCore 0:
  10.2 66.1 all-gather.11
  78.3 52.8 all-gather.9
  133.3 27.9 all-gather.13
  184.3 217.7 all-reduce.2
  404.1 103.5 all-gather.15
  509.7 56.2 all-gather.17
  577.2 301.3 all-gather.23
  911.4 54.2 all-gather.19
  1001.6 71.5 reduce-scatter.6
  1080.5 54.2 all-gather.21
  1137.1 100.1 reduce-scatter.14
  1239.4 55.9 reduce-scatter.16
  1297.7 26.9 reduce-scatter.12
  1326.9 58.9 reduce-scatter.10
  1389.1 71.3 reduce-scatter.8
